TPU v7x, 512 devices: a whole 4x8x8 slice. The times are simulated.
512 devices in a mesh: section: 4 (over x), rep: 128 (over y, z, core).
Axes of the slice: x: 4, y: 8, z: 8, core: 2. Of those that a mesh axis runs over, the one named last changes fastest.
Arguments:
- tile_features: bfloat16 [256, 16, 16, 512], P('rep'), may hold values from -6 to 6
- patches: bfloat16 [256, 16, 16, 768], P('rep'), may hold values from -6 to 6
- det_kernel: float32 [4, 7, 7, 512], P('section'), may hold values from -0.875 to 0.875
- det_gain: float32 [4, 512], P('section'), may hold values from 0.1 to 1.9
- det_in: bfloat16 [4, 512, 2048], P('section', None, 'rep'), may hold values from -0.25 to 0.25
- det_out: bfloat16 [4, 2048, 512], P('section', 'rep'), may hold values from -0.125 to 0.125
- det_scale: float32 [4, 512], P('section'), may hold values from 0.3 to 1.5
- cls_embed: bfloat16 [768, 1024], P(None, 'section'), may hold values from -0.21875 to 0.21875
- cls_merge: bfloat16 [512, 1024], P(None, 'section'), may hold values from -0.25 to 0.25
- cls_pos: bfloat16 [196, 1024], P(None, 'section'), may hold values from -3 to 3
- cls_qkv: bfloat16 [1024, 3, 512], P(None, None, 'section'), may hold values from -1.5 to 1.5
- cls_out: bfloat16 [512, 1024], P('section'), may hold values from -0.25 to 0.25
- cls_gain: float32 [2, 1024], replicated, may hold values from 0.1 to 1.9
- crop_plan: int32 [128, 4, 3, 3], P('rep'), may hold values from 0 to 2, as said below
- slot_from: int32 [128, 4], P('rep'), may hold values from 0 to 3, as said below
Outputs:
- crop_class: float32 [128, 4, 1024], P('rep', 'section')
Inputs may be any that keep to these rules, and one draw needn't show every extreme that they name: `crop_plan`: each entry is a micro-batch below 2 followed by a top and a left patch offset of 0 to 2; records that no slot names are arbitrary. `slot_from`: 0 marks an empty slot, 1 a crop from the replica one index lower, 2 the replica's own, 3 one from the replica one index higher; the first replica never has 1 and the last never has 3.
All inputs are finite; a program needn't handle non-finite values.
Results may differ from a plain program's by a relative error of at most 0.004.
Values may be sent and summed in bfloat16 or wider, within the bound.
No kernel may reach another device: no remote copies, remote signals or barrier semaphores. Data moves between devices by JAX's collectives and lax.ppermute only.
A program may use at most 64 MiB of HBM per device.

v0:
```python
import math
import jax
import jax.numpy as jnp
from jax import lax
from jax.sharding import PartitionSpec as P

HEAD_DIM = 64
TILE = 16
CROP = 14
epsilon = 1e-06


def passed_along(block, axis, distance):
    devices = range(lax.axis_size(axis))
    route = [(i - distance, i) for i in devices if i - distance in devices]
    return lax.ppermute(block, axis, route)


def spread(value, axis, source):
    kept = jnp.where(lax.axis_index(axis) == source, value, 0).astype(value.dtype)
    return lax.psum(kept, axis)


def padded_2(block, sides, width):
    for axis, dim in sides:
        count = lax.axis_size(axis)
        forward = [(i, i + 1) for i in range(count - 1)]
        backward = [(target, source) for source, target in forward]
        low = lax.ppermute(
            lax.slice_in_dim(block, block.shape[dim] - width, None, axis=dim), axis, forward
        )
        high = lax.ppermute(lax.slice_in_dim(block, 0, width, axis=dim), axis, backward)
        block = jnp.concatenate([low, block, high], axis=dim)
    return block


def layer_norm(values, gain_row):
    row_mean = jnp.mean(values, axis=-1, keepdims=True)
    centred = values - row_mean
    row_var = jnp.mean(centred * centred, axis=-1, keepdims=True)
    return centred * lax.rsqrt(row_var + epsilon) * gain_row


def detector_block(tile_rows, kernel, gain_row, in_weight, out_weight, scale_row):
    widened = tile_rows.astype(jnp.float32)
    padded = jnp.pad(widened, ((3, 3), (3, 3), (0, 0)))
    conv = jnp.zeros_like(widened)
    for row_shift in range(7):
        for col_shift in range(7):
            conv = (
                conv
                + padded[row_shift : row_shift + TILE, col_shift : col_shift + TILE]
                * kernel[row_shift, col_shift]
            )
    normed = layer_norm(conv, gain_row).astype(jnp.bfloat16).reshape(TILE * TILE, -1)
    hidden = jax.nn.gelu(jnp.dot(normed, in_weight, preferred_element_type=jnp.float32)).astype(
        jnp.bfloat16
    )
    update = jnp.dot(hidden, out_weight, preferred_element_type=jnp.float32).reshape(widened.shape)
    return (widened + scale_row * update).astype(jnp.bfloat16)


def per_device(
    tile_features,
    patches,
    det_kernel,
    det_gain,
    det_in,
    det_out,
    det_scale,
    cls_embed,
    cls_merge,
    cls_pos,
    cls_qkv,
    cls_out,
    cls_gain,
    crop_plan,
    slot_from,
):
    sections = lax.axis_size("section")
    section_num = lax.axis_index("section")
    micro_count = tile_features.shape[0]
    in_whole, out_whole = (
        lax.all_gather(det_in, "rep", axis=2, tiled=True),
        lax.all_gather(det_out, "rep", axis=1, tiled=True),
    )
    kernel = det_kernel[0]
    gain_row = det_gain[0]
    scale_row = det_scale[0]
    in_weight = in_whole[0]
    out_weight = out_whole[0]

    def run_block(operand_tile):
        return detector_block(operand_tile, kernel, gain_row, in_weight, out_weight, scale_row)

    def skip_block(operand_tile):
        return jnp.zeros_like(operand_tile)

    def tick(tick_index, loop_state):
        incoming, finals = loop_state
        micro_num = tick_index - section_num
        is_valid = (micro_num >= 0) & (micro_num < micro_count)
        clipped = jnp.clip(micro_num, 0, micro_count - 1)
        fresh_tile = lax.dynamic_index_in_dim(tile_features, clipped, 0, keepdims=False)
        operand = jnp.where(section_num == 0, fresh_tile, incoming)
        result = lax.cond(is_valid, run_block, skip_block, operand)
        stored = lax.dynamic_update_index_in_dim(finals, result, clipped, 0)
        finals = jnp.where(is_valid & (section_num == sections - 1), stored, finals)
        incoming = passed_along(result, "section", 1)
        return (incoming, finals)

    start_state = (
        jnp.zeros(tile_features.shape[1:], jnp.bfloat16),
        jnp.zeros(tile_features.shape, jnp.bfloat16),
    )
    unused_tile, finals = lax.fori_loop(0, micro_count + sections - 1, tick, start_state)
    finals = spread(finals, "section", sections - 1)
    pixel_width = patches.shape[3]
    feat_width = finals.shape[3]
    full_width = cls_gain.shape[1]
    local_width = cls_embed.shape[1]
    local_heads = cls_qkv.shape[2] // HEAD_DIM
    qkv_flat = cls_qkv.reshape(cls_qkv.shape[0], -1)
    gain_first = lax.dynamic_slice_in_dim(cls_gain[0], section_num * local_width, local_width)
    slot_plan = crop_plan[0]
    source = lax.dynamic_index_in_dim(slot_from[0], section_num, 0, keepdims=False)
    zero_index = jnp.int32(0)

    def cut_crop(record):
        pixel_rows = lax.dynamic_slice(
            patches, (record[0], record[1], record[2], zero_index), (1, CROP, CROP, pixel_width)
        ).reshape(CROP * CROP, pixel_width)
        feat_rows = lax.dynamic_slice(
            finals, (record[0], record[1], record[2], zero_index), (1, CROP, CROP, feat_width)
        ).reshape(CROP * CROP, feat_width)
        return (pixel_rows, feat_rows)

    pixel_rows, feat_rows = jax.vmap(cut_crop)(slot_plan.reshape(-1, 3))
    count = pixel_rows.shape[0]
    widened = (
        jnp.einsum("crp,pd->crd", pixel_rows, cls_embed, preferred_element_type=jnp.float32)
        + jnp.einsum("crp,pd->crd", feat_rows, cls_merge, preferred_element_type=jnp.float32)
        + cls_pos.astype(jnp.float32)[None]
    )
    row_sum, row_square = lax.psum(
        (jnp.sum(widened, axis=-1), jnp.sum(widened * widened, axis=-1)), "section"
    )
    row_mean = row_sum / full_width
    row_var = row_square / full_width - row_mean * row_mean
    attn_part = (
        (widened - row_mean[..., None]) * lax.rsqrt(row_var[..., None] + epsilon) * gain_first
    ).astype(jnp.bfloat16)
    attn_in = lax.all_gather(attn_part, "section", axis=2, tiled=True)
    qkv = jnp.einsum("crd,de->cre", attn_in, qkv_flat, preferred_element_type=jnp.float32).astype(
        jnp.bfloat16
    )
    qkv = qkv.reshape(count, CROP * CROP, 3, local_heads, HEAD_DIM)
    query_rows = qkv[:, :, 0]
    key_rows = qkv[:, :, 1]
    value_rows = qkv[:, :, 2]
    scores = jnp.einsum(
        "cqhd,ckhd->chqk", query_rows, key_rows, preferred_element_type=jnp.float32
    ) * (1.0 / math.sqrt(HEAD_DIM))
    top_score = jnp.max(scores, axis=-1, keepdims=True)
    weights = jnp.exp(scores - top_score)
    probs = (weights / jnp.sum(weights, axis=-1, keepdims=True)).astype(jnp.bfloat16)
    context = jnp.einsum(
        "chqk,ckhd->cqhd", probs, value_rows, preferred_element_type=jnp.float32
    ).astype(jnp.bfloat16)
    context_mean = jnp.mean(context.reshape(count, CROP * CROP, -1).astype(jnp.float32), axis=1)
    context_term = jnp.dot(
        context_mean, cls_out.astype(jnp.float32), precision=lax.Precision.HIGHEST
    )
    token_mean = jnp.mean(widened, axis=1)
    placed = lax.dynamic_update_slice_in_dim(
        jnp.zeros((count, full_width), jnp.float32), token_mean, section_num * local_width, 1
    )
    terms = (placed + context_term).reshape(sections, -1)
    pooled = lax.psum_scatter(terms, "section", scatter_dimension=0, tiled=True).reshape(
        -1, full_width
    )
    results = layer_norm(pooled, cls_gain[1])
    outgoing_results = jnp.stack([results[0], results[2]], axis=0)
    extended_results = padded_2(outgoing_results, (("rep", 0),), 1)
    result = jnp.where(
        source == 1, extended_results[0], jnp.where(source == 3, extended_results[3], results[1])
    )
    result = jnp.where(source == 0, jnp.zeros_like(result), result)
    return result[None, None, :]


def solution(mesh):
    return jax.shard_map(
        per_device,
        mesh=mesh,
        in_specs=(
            P("rep", None, None, None),
            P("rep", None, None, None),
            P("section", None, None, None),
            P("section", None),
            P("section", None, "rep"),
            P("section", "rep", None),
            P("section", None),
            P(None, "section"),
            P(None, "section"),
            P(None, "section"),
            P(None, None, "section"),
            P("section", None),
            P(),
            P("rep", None, None, None),
            P("rep", None),
        ),
        out_specs=P("rep", "section", None),
        check_vma=False,
    )
```

profile of v0, /device:TPU:32, one launch (start us, length us, event | category | flops | bytes accessed | tf_op | source)
XLA Modules:
  0.0 480.8 jit_solution(15910834706224890067)
XLA Ops:
  8.1 0.8 copy.37
  9.0 0.9 copy.64
  9.9 52.1 %while.18 = (s32[]{:T(128)}, bf16[2,16,16,768]{3,2,1,0:T(8,128)(2,1)}, s32[12,4]{0,1:T(4,128)S(1)}, bf16[12,1,14,14,768]{4,3,2,1,0:T(8,128)(2,1)}, s32[]{:T(128)}) while((s32[]{:T(128)}, bf16[2,16,16,768]{3,2,1,0:T(8,128)(2,1)}, s32[12,4]{0,1:T(4,128)S(1)}, bf16[12,1,14,14,768]{4,3,2,1,0:T(8,128)(2,1)}, s32[]{:T(128)}) %tuple.126), condition=%wide.while_cond, body=%wide.while_body.sunk | while | flops 2 | bytes 690297 | solution.py:130
  10.6 3.7 bitcast_dynamic-update-slice_fusion.2
  14.9 3.7 bitcast_dynamic-update-slice_fusion.2
  19.2 3.7 bitcast_dynamic-update-slice_fusion.2
  23.6 3.7 bitcast_dynamic-update-slice_fusion.2
  27.9 3.7 bitcast_dynamic-update-slice_fusion.2
  32.3 3.7 bitcast_dynamic-update-slice_fusion.2
  36.6 3.7 bitcast_dynamic-update-slice_fusion.2
  41.0 3.7 bitcast_dynamic-update-slice_fusion.2
  45.3 3.7 bitcast_dynamic-update-slice_fusion.2
  49.6 3.7 bitcast_dynamic-update-slice_fusion.2
  54.0 3.7 bitcast_dynamic-update-slice_fusion.2
  58.3 3.7 bitcast_dynamic-update-slice_fusion.2
  62.0 34.7 %all-gather.4.cloned.1.call-done = bf16[1,512,2048]{1,2,0:T(8,128)(2,1)} async-done(((bf16[1,512,16]{1,2,0:T(8,128)(2,1)}), bf16[1,512,2048]{1,2,0:T(8,128)(2,1)}) %all-gather.4.cloned.1.call-update) | async-done | bytes 2097168 | tf_op jit(solution)/shard_map/all_gather | solution.py:84
  96.7 4.0 copy.39
  100.7 79.0 %all-gather.6.cloned.1.call-done = bf16[1,2048,512]{2,1,0:T(8,128)(2,1)} async-done(((bf16[1,16,512]{2,1,0:T(8,128)(2,1)}), bf16[1,2048,512]{2,1,0:T(8,128)(2,1)}) %all-gather.6.cloned.1.call-update) | async-done | bytes 2097168 | tf_op jit(solution)/shard_map/all_gather | solution.py:85
  179.7 84.6 %while.17 = (s32[]{:T(128)}, bf16[16,16,512]{2,1,0:T(8,128)(2,1)S(1)}, bf16[2,16,16,512]{3,2,1,0:T(8,128)(2,1)S(1)}, s32[]{:T(128)}, pred[]{:T(512)}, /*index=5*...) while((s32[]{:T(128)}, ...), condition=%wide.region_5.6_spmd, body=%wide.region_0.5_spmd.sunk | while | flops 1093009664 | bytes 12373336 | solution.py:116
  179.8 10.3 %conditional.2 = (bf16[16,16,512]{2,1,0:T(8,128)(2,1)}, bf16[1,16,16,512]{3,2,1,0:T(8,128)(2,1)S(1)}) conditional(s32[]{:T(128)} %convert_element_type.74, () %tuple.120, (pred[]{:T(512)}, bf16[2,16,16,512]{3,2,1,0:T(8,128)(2,1)S(1)}, s32[]{:T(128)}, bf16[16,16,512]{2,1,0:T(8,128)(2,1)S(1)}, f32[1,512]{1,0:T(1,128)S(1)}, ...), branch_computations={%region_1.1_spmd, %region_2.4_spmd} | conditional | flops 1092878592 | bytes 10538005 | solution.py:106
  180.0 4.2 fusion.129
  184.6 3.8 fusion.8
  188.4 0.8 add_convert_fusion
  189.2 0.9 copy.68
  190.1 1.3 collective-permute-start
  191.5 6.5 %collective-permute-done = bf16[16,16,512]{2,1,0:T(8,128)(2,1)S(1)} collective-permute-done((bf16[16,16,512]{2,1,0:T(8,128)(2,1)}, bf16[16,16,512]{2,1,0:T(8,128)(2,1)S(1)}, u32[]{:S(2)}, u32[]{:S(2)}) %collective-permute-start) | collective-permute-done | bytes 262176 | tf_op jit(solution)/shard_map/while/body/eval_jaxpr/ppermute | solution.py:16
  198.0 10.3 %conditional.2 = (bf16[16,16,512]{2,1,0:T(8,128)(2,1)}, bf16[1,16,16,512]{3,2,1,0:T(8,128)(2,1)S(1)}) conditional(s32[]{:T(128)} %convert_element_type.74, () %tuple.120, (pred[]{:T(512)}, bf16[2,16,16,512]{3,2,1,0:T(8,128)(2,1)S(1)}, s32[]{:T(128)}, bf16[16,16,512]{2,1,0:T(8,128)(2,1)S(1)}, f32[1,512]{1,0:T(1,128)S(1)}, ...), branch_computations={%region_1.1_spmd, %region_2.4_spmd} | conditional | flops 1092878592 | bytes 10538005 | solution.py:106
  198.1 4.2 fusion.129
  202.8 3.8 fusion.8
  206.6 0.8 add_convert_fusion
  207.4 0.9 copy.68
  208.3 4.3 collective-permute-start
  212.7 5.7 %collective-permute-done = bf16[16,16,512]{2,1,0:T(8,128)(2,1)S(1)} collective-permute-done((bf16[16,16,512]{2,1,0:T(8,128)(2,1)}, bf16[16,16,512]{2,1,0:T(8,128)(2,1)S(1)}, u32[]{:S(2)}, u32[]{:S(2)}) %collective-permute-start) | collective-permute-done | bytes 262176 | tf_op jit(solution)/shard_map/while/body/eval_jaxpr/ppermute | solution.py:16
  218.4 0.7 conditional.2
  218.4 0.7 broadcast.139
  219.2 13.9 %collective-permute-start = (bf16[16,16,512]{2,1,0:T(8,128)(2,1)}, bf16[16,16,512]{2,1,0:T(8,128)(2,1)S(1)}, u32[]{:S(2)}, u32[]{:S(2)}) collective-permute-start(bf16[16,16,512]{2,1,0:T(8,128)(2,1)} %get-tuple-element.531), channel_id=1, source_target_pairs={{0,128},{128,256},{256,384},{1,129},{129,257},{257,385},{2,130},{1... | collective-permute-start | bytes 786440 | tf_op jit(solution)/shard_map/while/body/eval_jaxpr/ppermute | solution.py:16
  233.1 4.8 %collective-permute-done = bf16[16,16,512]{2,1,0:T(8,128)(2,1)S(1)} collective-permute-done((bf16[16,16,512]{2,1,0:T(8,128)(2,1)}, bf16[16,16,512]{2,1,0:T(8,128)(2,1)S(1)}, u32[]{:S(2)}, u32[]{:S(2)}) %collective-permute-start) | collective-permute-done | bytes 262176 | tf_op jit(solution)/shard_map/while/body/eval_jaxpr/ppermute | solution.py:16
  237.9 0.7 conditional.2
  237.9 0.7 broadcast.139
  238.7 4.3 collective-permute-start
  243.1 4.1 collective-permute-done
  247.2 0.7 conditional.2
  247.2 0.7 broadcast.139
  247.9 12.2 %collective-permute-start = (bf16[16,16,512]{2,1,0:T(8,128)(2,1)}, bf16[16,16,512]{2,1,0:T(8,128)(2,1)S(1)}, u32[]{:S(2)}, u32[]{:S(2)}) collective-permute-start(bf16[16,16,512]{2,1,0:T(8,128)(2,1)} %get-tuple-element.531), channel_id=1, source_target_pairs={{0,128},{128,256},{256,384},{1,129},{129,257},{257,385},{2,130},{1... | collective-permute-start | bytes 786440 | tf_op jit(solution)/shard_map/while/body/eval_jaxpr/ppermute | solution.py:16
  260.2 4.1 collective-permute-done
  264.3 1.5 broadcast_select_fusion
  266.1 6.0 %reshape.115 = bf16[12,196,768]{2,1,0:T(8,128)(2,1)} reshape(bf16[12,1,14,14,768]{4,3,2,1,0:T(8,128)(2,1)} %get-tuple-element.289) | data formatting | bytes 7225344 | tf_op jit(solution)/shard_map/vmap()/reshape | solution.py:132
  272.2 3.2 fusion.123
  275.3 52.9 %all-reduce.5.cloned.1.call-done = bf16[2,16,16,512]{3,0,2,1:T(2,128)(2,1)} async-done(((bf16[2,16,16,512]{3,0,2,1:T(2,128)(2,1)}), bf16[2,16,16,512]{3,0,2,1:T(2,128)(2,1)}) %all-reduce.5.cloned.1.call-update) | async-done | bytes 524304 | tf_op jit(solution)/shard_map/psum | solution.py:21
  328.2 12.1 %gather_fusion = bf16[12,14,14,512]{3,0,2,1:T(8,128)(2,1)} fusion(bf16[2,16,16,512]{3,0,2,1:T(2,128)(2,1)} %all-reduce.5.cloned.1.call-done, s32[12]{0:T(128)S(1)} %get-tuple-element.423), kind=kCustom, calls=%fused_computation | custom fusion | bytes 4817088 | tf_op jit(solution)/shard_map/vmap()/gather | solution.py:133
  340.3 6.5 %fusion.128 = (f32[12,256]{1,0:T(8,128)S(1)}, f32[12,196]{1,0:T(8,128)S(1)}, f32[12,196]{1,0:T(8,128)S(1)}, f32[12,196,256]{2,1,0:T(8,128)}) fusion(f32[196,256]{1,0:T(8,128)S(1)} %convert_element_type.50, f32[12,196,256]{2,1,0:T(8,128)S(1)} %fusion.123, bf16[512,256]{1,0:T(8,128)(2,1)S(1)} %copy-done.9, bf16[12,196,512]{2,0,1:T(8,128)(2,1)} %bitcast.131), kind=kOutput, calls=%fused_computation.214 | convolution fusion | flops 620167552 | bytes 7719296 | tf_op jit(solution)/shard_map/crp,pd->crd/dot_general | solution.py:142
  346.7 16.1 %all-reduce.2 = (f32[12,196]{1,0:T(8,128)S(1)}, f32[12,196]{1,0:T(8,128)S(1)}) all-reduce(f32[12,196]{1,0:T(8,128)S(1)} %get-tuple-element.327, f32[12,196]{1,0:T(8,128)S(1)} %get-tuple-element.328), channel_id=1, replica_groups=mesh['section'=4,'rep'=128] {'section'}, use_global_device_ids=true, to_apply=%region_10.11 | all-reduce | flops 4704 | bytes 37632 | tf_op jit(solution)/shard_map/psum | solution.py:145
  362.8 3.0 multiply_convert_fusion.1
  366.2 1.3 dynamic-slice.12
  367.5 61.6 %all-gather.8.cloned.1.call-done = bf16[12,196,1024]{2,1,0:T(8,128)(2,1)} async-done(((bf16[12,196,256]{2,1,0:T(8,128)(2,1)}), bf16[12,196,1024]{2,1,0:T(8,128)(2,1)}) %all-gather.8.cloned.1.call-update) | async-done | bytes 4816912 | tf_op jit(solution)/shard_map/all_gather | solution.py:153
  429.1 6.4 %convolution_convert_fusion = bf16[12,196,384]{2,1,0:T(8,128)(2,1)} fusion(bf16[12,196,1024]{2,1,0:T(8,128)(2,1)} %all-gather.8.cloned.1.call-done, bf16[1024,384,1]{0,1,2:T(8,128)(2,1)S(1)} %bitcast.133), kind=kOutput, calls=%fused_computation.181 | convolution fusion | flops 1850591232 | bytes 7409664 | tf_op jit(solution)/shard_map/crd,de->cre/dot_general | solution.py:154
  435.6 2.7 copy.44
  438.3 0.8 fusion.122
  439.1 4.1 fusion.137
  443.3 0.8 convert_reduce_fusion
  444.5 16.7 %all-reduce.1 = f32[4,3072]{1,0:T(4,128)S(1)} all-reduce(f32[4,3072]{1,0:T(4,128)S(1)} %reshape.119), channel_id=2, replica_groups=mesh['section'=4,'rep'=128] {'section'}, use_global_device_ids=true, to_apply=%region_15.16.clone | all-reduce | flops 12288 | bytes 98304
  462.3 1.9 collective-permute-start.1
  464.3 7.0 %collective-permute-start.2 = (f32[1,1024]{1,0:T(1,128)S(1)}, f32[1,1024]{1,0:T(1,128)S(1)}, u32[]{:S(2)}, u32[]{:S(2)}) collective-permute-start(f32[1,1024]{1,0:T(1,128)S(1)} %get-tuple-element.417), channel_id=1, source_target_pairs={{1,0},{2,1},{3,2},{4,3},{5,4},{6,5},{7,6},{8,7},{9,8},{10,9},{11,1... | collective-permute-start | bytes 12296 | tf_op jit(solution)/shard_map/ppermute | solution.py:32
  473.1 1.2 fusion.126
  (104 shorter events, 14.0 us)
Async XLA Ops:
  6.5 265.6 %copy-start = (bf16[768,256]{1,0:T(8,128)(2,1)S(1)}, bf16[768,256]{1,0:T(8,128)(2,1)}, u32[]{:S(2)}) copy-start(bf16[768,256]{1,0:T(8,128)(2,1)} %param.26) | copy-start | bytes 1179652
  6.5 90.1 %all-gather.4.cloned.1.call-start = ((), (), s32[]{:S(2)}) async-start(), calls=%async_computation | async-start | bytes 2113536 | tf_op jit(solution)/shard_map/all_gather | solution.py:84
  7.3 172.4 %all-gather.6.cloned.1.call-start = ((), (), s32[]{:S(2)}) async-start(), calls=%async_computation.1 | async-start | bytes 2113536 | tf_op jit(solution)/shard_map/all_gather | solution.py:85
  8.0 320.2 %all-reduce.5.cloned.1.call-start = ((), (), s32[]{:S(2)}) async-start(), calls=%async_computation.2 | async-start | bytes 1048576 | tf_op jit(solution)/shard_map/psum | solution.py:21
  96.7 83.1 %copy-start.1 = (bf16[2,16,16,512]{3,2,1,0:T(8,128)(2,1)S(1)}, bf16[2,16,16,512]{3,2,1,0:T(8,128)(2,1)}, u32[]{:S(2)}) copy-start(bf16[2,16,16,512]{3,2,1,0:T(8,128)(2,1)} %param.19) | copy-start | bytes 1572868
  96.7 83.1 %copy-start.5 = (f32[1,512]{1,0:T(1,128)S(1)}, f32[1,512]{1,0:T(1,128)}, u32[]{:S(2)}) copy-start(f32[1,512]{1,0:T(1,128)} %param.25) | copy-start | bytes 6148
  96.7 83.1 %copy-start.6 = (f32[1,512]{1,0:T(1,128)S(1)}, f32[1,512]{1,0:T(1,128)}, u32[]{:S(2)}) copy-start(f32[1,512]{1,0:T(1,128)} %param.22) | copy-start | bytes 6148
  179.7 86.3 %copy-start.7 = (f32[2,1024]{1,0:T(2,128)S(1)}, f32[2,1024]{1,0:T(2,128)}, u32[]{:S(2)}) copy-start(f32[2,1024]{1,0:T(2,128)} %param.31) | copy-start | bytes 24580
  190.1 7.9 %collective-permute-start = (bf16[16,16,512]{2,1,0:T(8,128)(2,1)}, bf16[16,16,512]{2,1,0:T(8,128)(2,1)S(1)}, u32[]{:S(2)}, u32[]{:S(2)}) collective-permute-start(bf16[16,16,512]{2,1,0:T(8,128)(2,1)} %get-tuple-element.531), channel_id=1, source_target_pairs={{0,128},{128,256},{256,384},{1,129},{129,257},{257,385},{2,130},{1... | collective-permute-start | bytes 786440 | tf_op jit(solution)/shard_map/while/body/eval_jaxpr/ppermute | solution.py:16
  208.3 10.1 %collective-permute-start = (bf16[16,16,512]{2,1,0:T(8,128)(2,1)}, bf16[16,16,512]{2,1,0:T(8,128)(2,1)S(1)}, u32[]{:S(2)}, u32[]{:S(2)}) collective-permute-start(bf16[16,16,512]{2,1,0:T(8,128)(2,1)} %get-tuple-element.531), channel_id=1, source_target_pairs={{0,128},{128,256},{256,384},{1,129},{129,257},{257,385},{2,130},{1... | collective-permute-start | bytes 786440 | tf_op jit(solution)/shard_map/while/body/eval_jaxpr/ppermute | solution.py:16
  219.2 18.8 %collective-permute-start = (bf16[16,16,512]{2,1,0:T(8,128)(2,1)}, bf16[16,16,512]{2,1,0:T(8,128)(2,1)S(1)}, u32[]{:S(2)}, u32[]{:S(2)}) collective-permute-start(bf16[16,16,512]{2,1,0:T(8,128)(2,1)} %get-tuple-element.531), channel_id=1, source_target_pairs={{0,128},{128,256},{256,384},{1,129},{129,257},{257,385},{2,130},{1... | collective-permute-start | bytes 786440 | tf_op jit(solution)/shard_map/while/body/eval_jaxpr/ppermute | solution.py:16
  238.7 8.5 %collective-permute-start = (bf16[16,16,512]{2,1,0:T(8,128)(2,1)}, bf16[16,16,512]{2,1,0:T(8,128)(2,1)S(1)}, u32[]{:S(2)}, u32[]{:S(2)}) collective-permute-start(bf16[16,16,512]{2,1,0:T(8,128)(2,1)} %get-tuple-element.531), channel_id=1, source_target_pairs={{0,128},{128,256},{256,384},{1,129},{129,257},{257,385},{2,130},{1... | collective-permute-start | bytes 786440 | tf_op jit(solution)/shard_map/while/body/eval_jaxpr/ppermute | solution.py:16
  247.9 16.4 %collective-permute-start = (bf16[16,16,512]{2,1,0:T(8,128)(2,1)}, bf16[16,16,512]{2,1,0:T(8,128)(2,1)S(1)}, u32[]{:S(2)}, u32[]{:S(2)}) collective-permute-start(bf16[16,16,512]{2,1,0:T(8,128)(2,1)} %get-tuple-element.531), channel_id=1, source_target_pairs={{0,128},{128,256},{256,384},{1,129},{129,257},{257,385},{2,130},{1... | collective-permute-start | bytes 786440 | tf_op jit(solution)/shard_map/while/body/eval_jaxpr/ppermute | solution.py:16
  265.8 163.3 %all-gather.8.cloned.1.call-start = ((), (), s32[]{:S(2)}) async-start(), calls=%async_computation.3 | async-start | bytes 6144000 | tf_op jit(solution)/shard_map/all_gather | solution.py:153
  266.1 6.0 %copy-start.4 = (bf16[196,256]{1,0:T(8,128)(2,1)S(1)}, bf16[196,256]{1,0:T(8,128)(2,1)}, u32[]{:S(2)}) copy-start(bf16[196,256]{1,0:T(8,128)(2,1)} %param.28) | copy-start | bytes 301060
  328.2 12.1 %copy-start.9 = (bf16[512,256]{1,0:T(8,128)(2,1)S(1)}, bf16[512,256]{1,0:T(8,128)(2,1)}, u32[]{:S(2)}) copy-start(bf16[512,256]{1,0:T(8,128)(2,1)} %param.27) | copy-start | bytes 786436
  362.8 3.1 copy-start.2
  443.3 1.0 copy-start.3
  443.3 28.0 %copy-start.8 = (s32[1,4]{1,0:T(1,128)S(1)}, s32[1,4]{1,0:T(1,128)}, u32[]{:S(2)}) copy-start(s32[1,4]{1,0:T(1,128)} %param.33) | copy-start | bytes 52
  462.3 10.8 %collective-permute-start.1 = (f32[1,1024]{1,0:T(1,128)S(1)}, f32[1,1024]{1,0:T(1,128)S(1)}, u32[]{:S(2)}, u32[]{:S(2)}) collective-permute-start(f32[1,1024]{1,0:T(1,128)S(1)} %get-tuple-element.418), channel_id=1, source_target_pairs={{0,1},{1,2},{2,3},{3,4},{4,5},{5,6},{6,7},{7,8},{8,9},{9,10},{10,1... | collective-permute-start | bytes 12296 | tf_op jit(solution)/shard_map/ppermute | solution.py:29
  464.3 8.9 %collective-permute-start.2 = (f32[1,1024]{1,0:T(1,128)S(1)}, f32[1,1024]{1,0:T(1,128)S(1)}, u32[]{:S(2)}, u32[]{:S(2)}) collective-permute-start(f32[1,1024]{1,0:T(1,128)S(1)} %get-tuple-element.417), channel_id=1, source_target_pairs={{1,0},{2,1},{3,2},{4,3},{5,4},{6,5},{7,6},{8,7},{9,8},{10,9},{11,1... | collective-permute-start | bytes 12296 | tf_op jit(solution)/shard_map/ppermute | solution.py:32
Sparse Core Ops, SparseCore 0:
  10.5 86.1 all-gather.3
  99.8 79.7 all-gather.5
  265.9 62.2 all-reduce.4
  366.0 63.1 all-gather.7
where the time goes:
time: 482 us; the launch traced here: 481 us
  waiting for transfers between devices  255 us (53%)
  local copies, waits for them, and re-layouts  85.6 us (18%)
  starting transfers between devices  45.1 us (9%)
  blocking collectives  32.7 us (7%)
  matrix products  25.5 us (5%)
  other arithmetic  22.2 us (5%)
  between operations  14.8 us (3%)
    all_gather x1, waiting for transfers between devices, per_device(): lax.all_gather(det_out, 'rep', axis=1, tiled=True)  79 us
    all_gather x1, waiting for transfers between devices, per_device(): attn_in = lax.all_gather(attn_part, 'section', axis=2, tiled=True)  61.6 us
    psum x1, waiting for transfers between devices, spread(): return lax.psum(kept, axis)  52.9 us
    gather x36, local copies, waits for them, and re-layouts  52 us
    ppermute x5, starting transfers between devices, passed_along(): return lax.ppermute(block, axis, route)  35.9 us
    all_gather x1, waiting for transfers between devices, per_device(): lax.all_gather(det_in, 'rep', axis=2, tiled=True)  34.7 us
    ppermute x5, waiting for transfers between devices, passed_along(): return lax.ppermute(block, axis, route)  25.1 us
    unnamed x1, blocking collectives  16.7 us
  transfers between devices with their start and end apart: 11, of which 9 were waited for; matrix products, arithmetic and copies ran while one was open for 15% of the time, Pallas kernels for 0%

commit v1 on v0

--- a/solution.py
+++ b/solution.py
@@ -81,7 +81,12 @@
     section_num = lax.axis_index("section")
     micro_count = tile_features.shape[0]
     in_whole, out_whole = (
-        lax.all_gather(det_in, "rep", axis=2, tiled=True),
+        jnp.concatenate(
+            lax.all_to_all(
+                jnp.stack([det_in for _ in range(lax.axis_size("rep"))], 0), "rep", 0, 0
+            ),
+            2,
+        ),
         lax.all_gather(det_out, "rep", axis=1, tiled=True),
     )
     kernel = det_kernel[0]

time: 482 us -> 457 us (0.948)
  waiting for transfers between devices: 255 us -> 190 us
  starting transfers between devices: 45.1 us -> 70.9 us
  local copies, waits for them, and re-layouts: 85.6 us -> 92.8 us
    all_gather x1 -> x0, waiting for transfers between devices: 34.7 us -> none  [per_device(): lax.all_gather(det_in, 'rep', axis=2, tiled=True)]
    all_gather x1, waiting for transfers between devices: 79 us -> 48.2 us  [per_device(): lax.all_gather(det_out, 'rep', axis=1, tiled=True)]
    all_to_all x0 -> x1, starting transfers between devices: none -> 17.5 us  [per_device(): lax.all_to_all(jnp.stack([det_in for _ in range(lax.axis_size('rep'))], 0...]
    ppermute x5, starting transfers between devices: 35.9 us -> 44.2 us  [passed_along(): return lax.ppermute(block, axis, route)]
    slice x6, local copies, waits for them, and re-layouts: 0.17 us -> 6.53 us  [detector_block(): kernel[row_shift, col_shift]]
  transfers between devices with their start and end apart: 11 -> 11, of which waited for: 9 -> 8; matrix products, arithmetic and copies ran while one was open for 15% -> 16% of each run, Pallas kernels for 0% -> 0%
where the time goes in v1:
time: 457 us; the launch traced here: 455 us
  waiting for transfers between devices  190 us (42%)
  local copies, waits for them, and re-layouts  92.8 us (20%)
  starting transfers between devices  70.9 us (16%)
  blocking collectives  32.7 us (7%)
  matrix products  29.1 us (6%)
  other arithmetic  24.1 us (5%)
  between operations  14.7 us (3%)
    all_gather x1, waiting for transfers between devices, per_device(): attn_in = lax.all_gather(attn_part, 'section', axis=2, tiled=True)  60.9 us
    psum x1, waiting for transfers between devices, spread(): return lax.psum(kept, axis)  55.4 us
    gather x36, local copies, waits for them, and re-layouts  53.4 us
    all_gather x1, waiting for transfers between devices, per_device(): lax.all_gather(det_out, 'rep', axis=1, tiled=True)  48.2 us
    ppermute x5, starting transfers between devices, passed_along(): return lax.ppermute(block, axis, route)  44.2 us
    ppermute x5, waiting for transfers between devices, passed_along(): return lax.ppermute(block, axis, route)  25.1 us
    all_to_all x1, starting transfers between devices, per_device(): lax.all_to_all(jnp.stack([det_in for _ in range(lax.axis_size('rep'))], 0...  17.5 us
    unnamed x1, blocking collectives  16.7 us
  transfers between devices with their start and end apart: 11, of which 8 were waited for; matrix products, arithmetic and copies ran while one was open for 16% of the time, Pallas kernels for 0%

profile of v1, /device:TPU:32, one launch (start us, length us, event | category | flops | bytes accessed | tf_op | source)
XLA Modules:
  0.0 455.0 jit_solution(10776315489887064994)
XLA Ops:
  6.5 2.4 stack.2
  8.9 17.5 %all-to-all-start = ((bf16[128,1,512,16]{2,3,1,0:T(8,128)(2,1)}), bf16[128,1,512,16]{2,3,1,0:T(8,128)(2,1)S(1)}, u32[]{:S(2)}, u32[]{:S(2)}) async-start(bf16[128,1,512,16]{2,3,1,0:T(8,128)(2,1)} %stack.2), calls=%async_computation | async-start | bytes 4194304 | tf_op jit(solution)/shard_map/all_to_all | solution.py:85
  28.1 53.4 %while.18 = (s32[]{:T(128)}, bf16[2,16,16,768]{3,2,1,0:T(8,128)(2,1)}, s32[12,4]{0,1:T(4,128)S(1)}, bf16[12,1,14,14,768]{4,3,2,1,0:T(8,128)(2,1)}, s32[]{:T(128)}) while((s32[]{:T(128)}, bf16[2,16,16,768]{3,2,1,0:T(8,128)(2,1)}, s32[12,4]{0,1:T(4,128)S(1)}, bf16[12,1,14,14,768]{4,3,2,1,0:T(8,128)(2,1)}, s32[]{:T(128)}) %tuple.126), condition=%wide.while_cond, body=%wide.while_body.sunk | while | flops 2 | bytes 690297 | solution.py:135
  28.8 3.8 bitcast_dynamic-update-slice_fusion.2
  33.2 3.8 bitcast_dynamic-update-slice_fusion.2
  37.7 3.8 bitcast_dynamic-update-slice_fusion.2
  42.1 3.8 bitcast_dynamic-update-slice_fusion.2
  46.6 3.8 bitcast_dynamic-update-slice_fusion.2
  51.0 3.8 bitcast_dynamic-update-slice_fusion.2
  55.5 3.8 bitcast_dynamic-update-slice_fusion.2
  60.0 3.8 bitcast_dynamic-update-slice_fusion.2
  64.4 3.8 bitcast_dynamic-update-slice_fusion.2
  68.8 3.8 bitcast_dynamic-update-slice_fusion.2
  73.3 3.8 bitcast_dynamic-update-slice_fusion.2
  77.7 3.8 bitcast_dynamic-update-slice_fusion.2
  81.5 2.5 copy.40
  84.0 48.2 %all-gather.3.cloned.1.call-done = bf16[1,2048,512]{2,1,0:T(8,128)(2,1)} async-done(((bf16[1,16,512]{2,1,0:T(8,128)(2,1)}), bf16[1,2048,512]{2,1,0:T(8,128)(2,1)}) %all-gather.3.cloned.1.call-update) | async-done | bytes 2097168 | tf_op jit(solution)/shard_map/all_gather | solution.py:90
  132.3 101.3 %while.17 = (s32[]{:T(128)}, bf16[16,16,512]{2,1,0:T(8,128)(2,1)S(1)}, bf16[2,16,16,512]{3,2,1,0:T(8,128)(2,1)S(1)}, s32[]{:T(128)}, pred[]{:T(512)}, /*index=5*...) while((s32[]{:T(128)}, ...), condition=%wide.region_5.6_spmd, body=%wide.region_0.5_spmd.sunk | while | flops 1093009664 | bytes 12373336 | solution.py:121
  132.3 14.5 %conditional.2 = (bf16[16,16,512]{2,1,0:T(8,128)(2,1)}, bf16[1,16,16,512]{3,2,1,0:T(8,128)(2,1)S(1)}) conditional(s32[]{:T(128)} %convert_element_type.74, () %tuple.120, (pred[]{:T(512)}, bf16[2,16,16,512]{3,2,1,0:T(8,128)(2,1)}, s32[]{:T(128)}, bf16[16,16,512]{2,1,0:T(8,128)(2,1)S(1)}, f32[1,512]{1,0:T(1,128)S(1)}, ...), branch_computations={%region_1.1_spmd, %region_2.4_spmd} | conditional | flops 1092878592 | bytes 10538005 | solution.py:111
  132.3 1.1 fusion.133
  133.4 1.2 fusion.132
  134.7 1.0 fusion.134
  135.6 1.0 fusion.106
  136.6 4.2 fusion.129
  141.2 3.8 fusion.8
  145.9 0.9 copy.69
  146.8 1.3 collective-permute-start
  148.2 6.5 %collective-permute-done = bf16[16,16,512]{2,1,0:T(8,128)(2,1)S(1)} collective-permute-done((bf16[16,16,512]{2,1,0:T(8,128)(2,1)}, bf16[16,16,512]{2,1,0:T(8,128)(2,1)S(1)}, u32[]{:S(2)}, u32[]{:S(2)}) %collective-permute-start) | collective-permute-done | bytes 262176 | tf_op jit(solution)/shard_map/while/body/eval_jaxpr/ppermute | solution.py:16
  154.7 14.5 %conditional.2 = (bf16[16,16,512]{2,1,0:T(8,128)(2,1)}, bf16[1,16,16,512]{3,2,1,0:T(8,128)(2,1)S(1)}) conditional(s32[]{:T(128)} %convert_element_type.74, () %tuple.120, (pred[]{:T(512)}, bf16[2,16,16,512]{3,2,1,0:T(8,128)(2,1)}, s32[]{:T(128)}, bf16[16,16,512]{2,1,0:T(8,128)(2,1)S(1)}, f32[1,512]{1,0:T(1,128)S(1)}, ...), branch_computations={%region_1.1_spmd, %region_2.4_spmd} | conditional | flops 1092878592 | bytes 10538005 | solution.py:111
  154.7 1.1 fusion.133
  155.8 1.2 fusion.132
  157.0 1.0 fusion.134
  158.0 1.0 fusion.106
  159.0 4.2 fusion.129
  163.6 3.8 fusion.8
  168.2 0.9 copy.69
  169.2 4.3 collective-permute-start
  173.6 5.7 %collective-permute-done = bf16[16,16,512]{2,1,0:T(8,128)(2,1)S(1)} collective-permute-done((bf16[16,16,512]{2,1,0:T(8,128)(2,1)}, bf16[16,16,512]{2,1,0:T(8,128)(2,1)S(1)}, u32[]{:S(2)}, u32[]{:S(2)}) %collective-permute-start) | collective-permute-done | bytes 262176 | tf_op jit(solution)/shard_map/while/body/eval_jaxpr/ppermute | solution.py:16
  180.0 18.0 %collective-permute-start = (bf16[16,16,512]{2,1,0:T(8,128)(2,1)}, bf16[16,16,512]{2,1,0:T(8,128)(2,1)S(1)}, u32[]{:S(2)}, u32[]{:S(2)}) collective-permute-start(bf16[16,16,512]{2,1,0:T(8,128)(2,1)} %get-tuple-element.531), channel_id=1, source_target_pairs={{0,128},{128,256},{256,384},{1,129},{129,257},{257,385},{2,130},{1... | collective-permute-start | bytes 786440 | tf_op jit(solution)/shard_map/while/body/eval_jaxpr/ppermute | solution.py:16
  198.1 4.8 %collective-permute-done = bf16[16,16,512]{2,1,0:T(8,128)(2,1)S(1)} collective-permute-done((bf16[16,16,512]{2,1,0:T(8,128)(2,1)}, bf16[16,16,512]{2,1,0:T(8,128)(2,1)S(1)}, u32[]{:S(2)}, u32[]{:S(2)}) %collective-permute-start) | collective-permute-done | bytes 262176 | tf_op jit(solution)/shard_map/while/body/eval_jaxpr/ppermute | solution.py:16
  203.7 4.3 collective-permute-start
  208.1 4.1 collective-permute-done
  213.0 16.4 %collective-permute-start = (bf16[16,16,512]{2,1,0:T(8,128)(2,1)}, bf16[16,16,512]{2,1,0:T(8,128)(2,1)S(1)}, u32[]{:S(2)}, u32[]{:S(2)}) collective-permute-start(bf16[16,16,512]{2,1,0:T(8,128)(2,1)} %get-tuple-element.531), channel_id=1, source_target_pairs={{0,128},{128,256},{256,384},{1,129},{129,257},{257,385},{2,130},{1... | collective-permute-start | bytes 786440 | tf_op jit(solution)/shard_map/while/body/eval_jaxpr/ppermute | solution.py:16
  229.5 4.1 collective-permute-done
  233.6 1.4 broadcast_select_fusion
  235.3 6.1 %reshape.121 = bf16[12,196,768]{2,1,0:T(8,128)(2,1)} reshape(bf16[12,1,14,14,768]{4,3,2,1,0:T(8,128)(2,1)} %get-tuple-element.289) | data formatting | bytes 7225344 | tf_op jit(solution)/shard_map/vmap()/reshape | solution.py:137
  241.4 4.6 %fusion.123 = f32[12,196,256]{2,1,0:T(8,128)} fusion(bf16[12,196,768]{2,1,0:T(8,128)(2,1)} %reshape.121, bf16[768,256]{1,0:T(8,128)(2,1)S(1)} %copy-done), kind=kOutput, calls=%fused_computation.189 | convolution fusion | flops 924844032 | bytes 6414336 | tf_op jit(solution)/shard_map/crp,pd->crd/dot_general | solution.py:146
  246.0 55.4 %all-reduce.5.cloned.1.call-done = bf16[2,16,16,512]{3,0,2,1:T(2,128)(2,1)} async-done(((bf16[2,16,16,512]{3,0,2,1:T(2,128)(2,1)}), bf16[2,16,16,512]{3,0,2,1:T(2,128)(2,1)}) %all-reduce.5.cloned.1.call-update) | async-done | bytes 524304 | tf_op jit(solution)/shard_map/psum | solution.py:21
  301.4 11.1 %gather_fusion = bf16[12,14,14,512]{3,0,2,1:T(8,128)(2,1)} fusion(bf16[2,16,16,512]{3,0,2,1:T(2,128)(2,1)} %all-reduce.5.cloned.1.call-done, s32[12]{0:T(128)S(1)} %get-tuple-element.423), kind=kCustom, calls=%fused_computation | custom fusion | bytes 4817088 | tf_op jit(solution)/shard_map/vmap()/gather | solution.py:138
  312.5 7.2 %fusion.128 = (f32[12,256]{1,0:T(8,128)S(1)}, f32[12,196]{1,0:T(8,128)S(1)}, f32[12,196]{1,0:T(8,128)S(1)}, f32[12,196,256]{2,1,0:T(8,128)}) fusion(f32[196,256]{1,0:T(8,128)S(1)} %convert_element_type.50, f32[12,196,256]{2,1,0:T(8,128)} %fusion.123, bf16[512,256]{1,0:T(8,128)(2,1)S(1)} %copy-done.10, bf16[12,196,512]{2,0,1:T(8,128)(2,1)} %bitcast.137), kind=kOutput, calls=%fused_computation.214 | convolution fusion | flops 620167552 | bytes 7719296 | tf_op jit(solution)/shard_map/crp,pd->crd/dot_general | solution.py:147
  319.7 16.1 %all-reduce.2 = (f32[12,196]{1,0:T(8,128)S(1)}, f32[12,196]{1,0:T(8,128)S(1)}) all-reduce(f32[12,196]{1,0:T(8,128)S(1)} %get-tuple-element.327, f32[12,196]{1,0:T(8,128)S(1)} %get-tuple-element.328), channel_id=1, replica_groups=mesh['section'=4,'rep'=128] {'section'}, use_global_device_ids=true, to_apply=%region_10.11 | all-reduce | flops 4704 | bytes 37632 | tf_op jit(solution)/shard_map/psum | solution.py:150
  335.8 3.0 multiply_convert_fusion.1
  338.9 1.2 copy.43
  340.0 1.3 dynamic-slice.12
  341.3 60.9 %all-gather.5.cloned.1.call-done = bf16[12,196,1024]{2,1,0:T(8,128)(2,1)} async-done(((bf16[12,196,256]{2,1,0:T(8,128)(2,1)}), bf16[12,196,1024]{2,1,0:T(8,128)(2,1)}) %all-gather.5.cloned.1.call-update) | async-done | bytes 4816912 | tf_op jit(solution)/shard_map/all_gather | solution.py:158
  402.2 5.4 %convolution_convert_fusion = bf16[12,196,384]{2,1,0:T(8,128)(2,1)S(1)} fusion(bf16[12,196,1024]{2,1,0:T(8,128)(2,1)} %all-gather.5.cloned.1.call-done, bf16[1024,384,1]{0,1,2:T(8,128)(2,1)} %bitcast.138), kind=kOutput, calls=%fused_computation.181 | convolution fusion | flops 1850591232 | bytes 7409664 | tf_op jit(solution)/shard_map/crd,de->cre/dot_general | solution.py:159
  407.6 2.5 copy.45
  410.1 2.2 fusion.122
  412.3 4.1 fusion.137
  416.4 1.9 convert_reduce_fusion
  418.7 16.7 %all-reduce.1 = f32[4,3072]{1,0:T(4,128)S(1)} all-reduce(f32[4,3072]{1,0:T(4,128)S(1)} %reshape.126), channel_id=2, replica_groups=mesh['section'=4,'rep'=128] {'section'}, use_global_device_ids=true, to_apply=%region_15.16.clone | all-reduce | flops 12288 | bytes 98304
  436.5 1.9 collective-permute-start.1
  438.4 7.0 %collective-permute-start.2 = (f32[1,1024]{1,0:T(1,128)S(1)}, f32[1,1024]{1,0:T(1,128)S(1)}, u32[]{:S(2)}, u32[]{:S(2)}) collective-permute-start(f32[1,1024]{1,0:T(1,128)S(1)} %get-tuple-element.417), channel_id=1, source_target_pairs={{1,0},{2,1},{3,2},{4,3},{5,4},{6,5},{7,6},{8,7},{9,8},{10,9},{11,1... | collective-permute-start | bytes 12296 | tf_op jit(solution)/shard_map/ppermute | solution.py:32
  447.3 1.2 fusion.126
  (106 shorter events, 19.5 us)
Async XLA Ops:
  6.5 234.9 %copy-start = (bf16[768,256]{1,0:T(8,128)(2,1)S(1)}, bf16[768,256]{1,0:T(8,128)(2,1)}, u32[]{:S(2)}) copy-start(bf16[768,256]{1,0:T(8,128)(2,1)} %param.26) | copy-start | bytes 1179652
  8.9 18.3 %copy-start.8 = (s32[1,4,3,3]{1,0,3,2:T(1,128)S(1)}, s32[1,4,3,3]{1,0,3,2:T(1,128)}, u32[]{:S(2)}) copy-start(s32[1,4,3,3]{1,0,3,2:T(1,128)} %param.32) | copy-start | bytes 436
  8.9 18.5 %copy-start.4 = (f32[1,7,7,512]{3,0,2,1:T(1,128)S(1)}, f32[1,7,7,512]{3,0,2,1:T(1,128)}, u32[]{:S(2)}) copy-start(f32[1,7,7,512]{3,0,2,1:T(1,128)} %param.21) | copy-start | bytes 301060
  8.9 72.6 %all-to-all-start = ((bf16[128,1,512,16]{2,3,1,0:T(8,128)(2,1)}), bf16[128,1,512,16]{2,3,1,0:T(8,128)(2,1)S(1)}, u32[]{:S(2)}, u32[]{:S(2)}) async-start(bf16[128,1,512,16]{2,3,1,0:T(8,128)(2,1)} %stack.2), calls=%async_computation | async-start | bytes 4194304 | tf_op jit(solution)/shard_map/all_to_all | solution.py:85
  26.4 105.8 %all-gather.3.cloned.1.call-start = ((), (), s32[]{:S(2)}) async-start(), calls=%async_computation.1 | async-start | bytes 2113536 | tf_op jit(solution)/shard_map/all_gather | solution.py:90
  27.1 274.3 %all-reduce.5.cloned.1.call-start = ((), (), s32[]{:S(2)}) async-start(), calls=%async_computation.2 | async-start | bytes 1048576 | tf_op jit(solution)/shard_map/psum | solution.py:21
  81.5 50.7 %copy-start.5 = (f32[1,512]{1,0:T(1,128)S(1)}, f32[1,512]{1,0:T(1,128)}, u32[]{:S(2)}) copy-start(f32[1,512]{1,0:T(1,128)} %param.25) | copy-start | bytes 6148
  81.5 50.8 %copy-start.6 = (f32[1,512]{1,0:T(1,128)S(1)}, f32[1,512]{1,0:T(1,128)}, u32[]{:S(2)}) copy-start(f32[1,512]{1,0:T(1,128)} %param.22) | copy-start | bytes 6148
  132.3 103.0 %copy-start.7 = (f32[2,1024]{1,0:T(2,128)S(1)}, f32[2,1024]{1,0:T(2,128)}, u32[]{:S(2)}) copy-start(f32[2,1024]{1,0:T(2,128)} %param.31) | copy-start | bytes 24580
  146.8 7.9 %collective-permute-start = (bf16[16,16,512]{2,1,0:T(8,128)(2,1)}, bf16[16,16,512]{2,1,0:T(8,128)(2,1)S(1)}, u32[]{:S(2)}, u32[]{:S(2)}) collective-permute-start(bf16[16,16,512]{2,1,0:T(8,128)(2,1)} %get-tuple-element.531), channel_id=1, source_target_pairs={{0,128},{128,256},{256,384},{1,129},{129,257},{257,385},{2,130},{1... | collective-permute-start | bytes 786440 | tf_op jit(solution)/shard_map/while/body/eval_jaxpr/ppermute | solution.py:16
  169.2 10.1 %collective-permute-start = (bf16[16,16,512]{2,1,0:T(8,128)(2,1)}, bf16[16,16,512]{2,1,0:T(8,128)(2,1)S(1)}, u32[]{:S(2)}, u32[]{:S(2)}) collective-permute-start(bf16[16,16,512]{2,1,0:T(8,128)(2,1)} %get-tuple-element.531), channel_id=1, source_target_pairs={{0,128},{128,256},{256,384},{1,129},{129,257},{257,385},{2,130},{1... | collective-permute-start | bytes 786440 | tf_op jit(solution)/shard_map/while/body/eval_jaxpr/ppermute | solution.py:16
  180.0 22.9 %collective-permute-start = (bf16[16,16,512]{2,1,0:T(8,128)(2,1)}, bf16[16,16,512]{2,1,0:T(8,128)(2,1)S(1)}, u32[]{:S(2)}, u32[]{:S(2)}) collective-permute-start(bf16[16,16,512]{2,1,0:T(8,128)(2,1)} %get-tuple-element.531), channel_id=1, source_target_pairs={{0,128},{128,256},{256,384},{1,129},{129,257},{257,385},{2,130},{1... | collective-permute-start | bytes 786440 | tf_op jit(solution)/shard_map/while/body/eval_jaxpr/ppermute | solution.py:16
  203.7 8.5 %collective-permute-start = (bf16[16,16,512]{2,1,0:T(8,128)(2,1)}, bf16[16,16,512]{2,1,0:T(8,128)(2,1)S(1)}, u32[]{:S(2)}, u32[]{:S(2)}) collective-permute-start(bf16[16,16,512]{2,1,0:T(8,128)(2,1)} %get-tuple-element.531), channel_id=1, source_target_pairs={{0,128},{128,256},{256,384},{1,129},{129,257},{257,385},{2,130},{1... | collective-permute-start | bytes 786440 | tf_op jit(solution)/shard_map/while/body/eval_jaxpr/ppermute | solution.py:16
  213.0 20.6 %collective-permute-start = (bf16[16,16,512]{2,1,0:T(8,128)(2,1)}, bf16[16,16,512]{2,1,0:T(8,128)(2,1)S(1)}, u32[]{:S(2)}, u32[]{:S(2)}) collective-permute-start(bf16[16,16,512]{2,1,0:T(8,128)(2,1)} %get-tuple-element.531), channel_id=1, source_target_pairs={{0,128},{128,256},{256,384},{1,129},{129,257},{257,385},{2,130},{1... | collective-permute-start | bytes 786440 | tf_op jit(solution)/shard_map/while/body/eval_jaxpr/ppermute | solution.py:16
  235.0 167.2 %all-gather.5.cloned.1.call-start = ((), (), s32[]{:S(2)}) async-start(), calls=%async_computation.3 | async-start | bytes 6144000 | tf_op jit(solution)/shard_map/all_gather | solution.py:158
  235.3 6.1 %copy-start.3 = (bf16[196,256]{1,0:T(8,128)(2,1)S(1)}, bf16[196,256]{1,0:T(8,128)(2,1)}, u32[]{:S(2)}) copy-start(bf16[196,256]{1,0:T(8,128)(2,1)} %param.28) | copy-start | bytes 301060
  301.4 11.1 %copy-start.10 = (bf16[512,256]{1,0:T(8,128)(2,1)S(1)}, bf16[512,256]{1,0:T(8,128)(2,1)}, u32[]{:S(2)}) copy-start(bf16[512,256]{1,0:T(8,128)(2,1)} %param.27) | copy-start | bytes 786436
  335.8 3.1 copy-start.1
  416.4 2.1 copy-start.2
  416.4 29.0 %copy-start.9 = (s32[1,4]{1,0:T(1,128)S(1)}, s32[1,4]{1,0:T(1,128)}, u32[]{:S(2)}) copy-start(s32[1,4]{1,0:T(1,128)} %param.33) | copy-start | bytes 52
  436.5 10.8 %collective-permute-start.1 = (f32[1,1024]{1,0:T(1,128)S(1)}, f32[1,1024]{1,0:T(1,128)S(1)}, u32[]{:S(2)}, u32[]{:S(2)}) collective-permute-start(f32[1,1024]{1,0:T(1,128)S(1)} %get-tuple-element.418), channel_id=1, source_target_pairs={{0,1},{1,2},{2,3},{3,4},{4,5},{5,6},{6,7},{7,8},{8,9},{9,10},{10,1... | collective-permute-start | bytes 12296 | tf_op jit(solution)/shard_map/ppermute | solution.py:29
  438.4 8.9 %collective-permute-start.2 = (f32[1,1024]{1,0:T(1,128)S(1)}, f32[1,1024]{1,0:T(1,128)S(1)}, u32[]{:S(2)}, u32[]{:S(2)}) collective-permute-start(f32[1,1024]{1,0:T(1,128)S(1)} %get-tuple-element.417), channel_id=1, source_target_pairs={{1,0},{2,1},{3,2},{4,3},{5,4},{6,5},{7,6},{8,7},{9,8},{10,9},{11,1... | collective-permute-start | bytes 12296 | tf_op jit(solution)/shard_map/ppermute | solution.py:32
Sparse Core Ops, SparseCore 0:
  30.4 101.7 all-gather.2
  235.1 66.2 all-reduce.4
  339.0 63.2 all-gather.4
